TPU v7x, 32 devices: a whole 2x2x4 slice. The times are simulated.
32 devices in a mesh: seq: 4 (over z), head: 8 (over y, x, core).
Axes of the slice: x: 2, y: 2, z: 4, core: 2. Of those that a mesh axis runs over, the one named last changes fastest.
Arguments:
- lengths: int32 [16], replicated, may hold values from 128 to 8192, as said below
- page_owner: int32 [384], replicated, may hold values from 0 to 16, as said below
- page_index: int32 [384], replicated, may hold values from 0 to 127, as said below
- page_dest: int32 [384], replicated, may hold values from 0 to 383, as said below
- src_cache: bfloat16 [384, 8, 64, 256], P(('seq', 'head')), may hold values from -8 to 8
- queries: bfloat16 [2, 16, 4096], replicated, may hold values from -8 to 8
- new_kv: bfloat16 [2, 16, 8, 256], replicated, may hold values from -6 to 6
- hidden_in: bfloat16 [2, 16, 4096], P(None, None, ('seq', 'head')), may hold values from -60 to 60
- out_weight: bfloat16 [4096, 4096], P(None, ('seq', 'head')), may hold values from -1.5 to 1.5
- norm_gain: bfloat16 [4096], P(('seq', 'head')), may hold values from 0.099609375 to 1.8984375
- router: bfloat16 [4096, 8], P(('seq', 'head')), may hold values from -0.09375 to 0.09375
- routes: int32 [2, 16, 2], replicated, may hold values from 0 to 7, all different within a row
- w_gate: bfloat16 [8, 4096, 8192], P('seq', None, 'head'), may hold values from -0.09375 to 0.09375
- w_up: bfloat16 [8, 4096, 8192], P('seq', None, 'head'), may hold values from -0.09375 to 0.09375
- w_down: bfloat16 [8, 8192, 4096], P('seq', 'head'), may hold values from -0.0625 to 0.0625
Outputs:
- page_pool: bfloat16 [8, 384, 64, 256], P('head', 'seq')
- mixed: bfloat16 [2, 16, 4096], P(None, None, ('seq', 'head'))
Inputs may be any that keep to these rules, and one draw needn't show every extreme that they name: Each length is at least 128; one equals 8192; the requests' pages, lengths[r] / 64 rounded up for request r, fit into the 384 pages. `page_owner`: request r owns exactly lengths[r] / 64 rounded up source pages; the other pages carry 16. `page_index`: the pages of request r carry 0 to their count minus 1, each once; pages without request carry 0. `page_dest`: A permutation. Slot g belongs to destination group ((g % 384) // 96) + g // 384. Of the 12 pages that one device holds (pages i * 12 to (i + 1) * 12 - 1), at most 3 go to one group, and every draw has a device that sends exactly 3 to some group.
All inputs are finite; a program needn't handle non-finite values.
Results may differ from a plain program's by a relative error of at most 0.009.
Values may be sent and summed in bfloat16 or wider, within the bound.
No kernel may reach another device: no remote copies, remote signals or barrier semaphores. Data moves between devices by JAX's collectives and lax.ppermute only.
A program may use at most 128 MiB of HBM per device.

v0:
```python
import jax
import jax.numpy as jnp
from jax import lax
from jax.sharding import PartitionSpec as P

D = 4096
HQ = 32
KVH = 8
HD = 128
TOPK = 2
PAGE = 64
REQS = 16
NEG_FILL = -1e30
EPSILON = 1e-05
HIGHEST = lax.Precision.HIGHEST


def joined(array, axis, combine):
    everything = jax.tree.map(lambda part: lax.all_gather(part, axis), array)
    initial = jax.tree.map(lambda part: part[0], everything)

    def hop(k, so_far):
        return combine(so_far, jax.tree.map(lambda part: part[k], everything))

    return lax.fori_loop(1, lax.axis_size(axis), hop, initial)


def gate_mix(logits, picked):
    expert_ids = jnp.arange(logits.shape[1], dtype=jnp.int32)[None, :]
    first_hit = picked[:, 0:1] == expert_ids
    second_hit = picked[:, 1:2] == expert_ids
    first_logit = jnp.sum(jnp.where(first_hit, logits, 0.0), axis=1)
    second_logit = jnp.sum(jnp.where(second_hit, logits, 0.0), axis=1)
    leading = 1.0 / (1.0 + jnp.exp(second_logit - first_logit))
    trailing = 1.0 / (1.0 + jnp.exp(first_logit - second_logit))
    return jnp.where(first_hit, leading[:, None], 0.0) + jnp.where(
        second_hit, trailing[:, None], 0.0
    )


def combine(earlier, later):
    first_top, first_sum, first_acc = earlier
    second_top, second_sum, second_acc = later
    joint_top = jnp.maximum(first_top, second_top)
    first_factor = jnp.exp(first_top - joint_top)
    second_factor = jnp.exp(second_top - joint_top)
    return (
        joint_top,
        first_sum * first_factor + second_sum * second_factor,
        first_acc * first_factor[..., None] + second_acc * second_factor[..., None],
    )


def slot_plan(page_dest, pages_dev, slot_count, slots_dev, replicas, groups):
    part_index = page_dest // slot_count
    within = page_dest % slot_count
    target = within // slots_dev * replicas + part_index
    position = within % slots_dev
    per_device = target.reshape(-1, pages_dev)
    onehot = (per_device[:, :, None] == jnp.arange(groups, dtype=jnp.int32)[None, None, :]).astype(
        jnp.int32
    )
    before = jnp.cumsum(onehot, axis=1) - onehot
    ranking = jnp.sum(before * onehot, axis=2).reshape(-1)
    return (target, position, ranking)


def partial_attention(page_block, owners, page_pos, lengths, grouped, score_scale):
    head_dim = grouped.shape[-1]
    page_len = page_block.shape[2]
    requests = grouped.shape[1]
    clipped = jnp.minimum(owners, requests - 1)
    length_cap = jnp.take(lengths, clipped)
    offsets = page_pos[:, None] * page_len + jnp.arange(page_len, dtype=jnp.int32)[None, :]
    is_live = (owners < requests)[:, None] & (offsets < length_cap[:, None])
    live_mask = is_live[None, :, None, None, :]
    asked_rows = jnp.take(grouped, clipped, axis=1)
    scores = (
        jnp.einsum(
            "spkgd,pktd->spkgt",
            asked_rows,
            page_block[..., :head_dim],
            preferred_element_type=jnp.float32,
        )
        * score_scale
    )
    scores = jnp.where(live_mask, scores, NEG_FILL)
    members = owners[:, None] == jnp.arange(requests, dtype=jnp.int32)[None, :]
    page_top = jnp.max(scores, axis=4)
    row_top = jnp.max(
        jnp.where(members[None, :, :, None, None], page_top[:, :, None], NEG_FILL), axis=1
    )
    weights = jnp.where(
        live_mask, jnp.exp(scores - jnp.take(row_top, clipped, axis=1)[..., None]), 0.0
    )
    member_mask = members.astype(jnp.float32)
    totals = jnp.einsum("pr,spkg->srkg", member_mask, jnp.sum(weights, axis=4), precision=HIGHEST)
    page_out = jnp.einsum(
        "spkgt,pktd->spkgd",
        weights.astype(jnp.bfloat16),
        page_block[..., head_dim:],
        preferred_element_type=jnp.float32,
    )
    weighted = jnp.einsum("pr,spkgd->srkgd", member_mask, page_out, precision=HIGHEST)
    return (row_top, totals, weighted)


def body(
    lengths,
    page_owner,
    page_index,
    page_dest,
    src_cache,
    queries,
    new_kv,
    hidden_in,
    out_weight,
    norm_gain,
    router,
    routes,
    w_gate,
    w_up,
    w_down,
):
    seq_count = lax.axis_size("seq")
    head_count = lax.axis_size("head")
    device_count = seq_count * head_count
    seq_pos = lax.axis_index("seq")
    head_pos = lax.axis_index("head")
    pages_dev = src_cache.shape[0]
    page_total = page_dest.shape[0]
    replicas = head_count // KVH
    groups = seq_count * replicas
    slot_count = page_total // replicas
    slots_dev = pages_dev * KVH
    capacity = (slots_dev + device_count - 1) // device_count
    group_size = HQ // KVH
    step_count = queries.shape[0]
    row_count = step_count * REQS
    source = seq_pos * head_count + head_pos
    target, position, ranking = slot_plan(
        page_dest, pages_dev, slot_count, slots_dev, replicas, groups
    )
    local_target = lax.dynamic_slice_in_dim(target, source * pages_dev, pages_dev)
    local_rank = lax.dynamic_slice_in_dim(ranking, source * pages_dev, pages_dev)
    wanted = jnp.arange(groups * capacity, dtype=jnp.int32)
    matches = (local_target[None, :] == (wanted // capacity)[:, None]) & (
        local_rank[None, :] == (wanted % capacity)[:, None]
    )
    picked_page = jnp.sum(
        jnp.where(matches, jnp.arange(pages_dev, dtype=jnp.int32)[None, :], 0), axis=1
    )
    filled = jnp.any(matches, axis=1)
    packed = jnp.where(
        filled[:, None, None, None],
        jnp.take(src_cache, picked_page, axis=0),
        jnp.zeros((), jnp.bfloat16),
    )
    packed = packed.reshape(seq_count, replicas, capacity, KVH, PAGE, 2 * HD).transpose(
        0, 3, 1, 2, 4, 5
    )
    arrived = lax.all_to_all(
        packed.reshape(device_count, capacity, PAGE, 2 * HD),
        ("seq", "head"),
        split_axis=0,
        concat_axis=0,
        tiled=True,
    )
    arrived = arrived.reshape(device_count * capacity, PAGE, 2 * HD)
    my_group = seq_pos * replicas + head_pos % replicas
    slot_ids = jnp.arange(slots_dev, dtype=jnp.int32)
    holders = (target[None, :] == my_group) & (position[None, :] == slot_ids[:, None])
    flat_index = jnp.arange(page_total, dtype=jnp.int32) // pages_dev * capacity + ranking
    chosen = jnp.sum(jnp.where(holders, flat_index[None, :], 0), axis=1)
    page_pool = jnp.take(arrived, chosen, axis=0)
    grouped = queries.reshape(step_count, REQS, KVH, group_size, HD)
    score_scale = HD ** (-0.5)
    owners = lax.dynamic_slice_in_dim(page_owner, source * pages_dev, pages_dev)
    places = lax.dynamic_slice_in_dim(page_index, source * pages_dev, pages_dev)
    row_top, totals, weighted = partial_attention(
        src_cache, owners, places, lengths, grouped, score_scale
    )
    row_top, totals, weighted = joined(
        (
            row_top.reshape(step_count, REQS, HQ),
            totals.reshape(step_count, REQS, HQ),
            weighted.reshape(step_count, REQS, HQ, HD),
        ),
        ("seq", "head"),
        combine,
    )
    fresh_scores = (
        jnp.einsum(
            "srkgd,urkd->srkgu", grouped, new_kv[..., :HD], preferred_element_type=jnp.float32
        )
        * score_scale
    )
    causal = (jnp.arange(step_count)[:, None] >= jnp.arange(step_count)[None, :])[:, None, None, :]
    fresh_scores = jnp.where(
        causal, fresh_scores.reshape(step_count, REQS, HQ, step_count), NEG_FILL
    )
    joint_top = jnp.maximum(row_top, jnp.max(fresh_scores, axis=3))
    factor = jnp.exp(row_top - joint_top)
    fresh_weights = jnp.where(causal, jnp.exp(fresh_scores - joint_top[..., None]), 0.0)
    totals = totals * factor + jnp.sum(fresh_weights, axis=3)
    fresh_rounded = fresh_weights.reshape(step_count, REQS, KVH, group_size, step_count).astype(
        jnp.bfloat16
    )
    fresh_out = jnp.einsum(
        "srkgu,urkd->srkgd", fresh_rounded, new_kv[..., HD:], preferred_element_type=jnp.float32
    )
    weighted = weighted * factor[..., None] + fresh_out.reshape(step_count, REQS, HQ, HD)
    attended = (weighted / totals[..., None]).reshape(row_count, HQ * HD).astype(jnp.bfloat16)
    attn_out = jnp.dot(attended, out_weight, preferred_element_type=jnp.float32)
    middle = hidden_in.reshape(row_count, -1).astype(jnp.float32) + attn_out
    gain_row = norm_gain.astype(jnp.float32)[None, :]
    squares, routed = lax.psum(
        (
            jnp.sum(middle * middle, axis=1),
            jnp.dot(middle * gain_row, router.astype(jnp.float32), precision=HIGHEST),
        ),
        ("seq", "head"),
    )
    inverse_rms = lax.rsqrt(squares / D + EPSILON)
    logits = routed * inverse_rms[:, None]
    normed = (middle * inverse_rms[:, None] * gain_row).astype(jnp.bfloat16)
    features = lax.all_gather(normed, ("seq", "head"), axis=1, tiled=True)
    mixture = gate_mix(logits, routes.reshape(row_count, TOPK))
    local_experts = w_gate.shape[0]
    local_mix = lax.dynamic_slice_in_dim(mixture, seq_pos * local_experts, local_experts, axis=1)
    gate_act = jnp.einsum("rd,edf->erf", features, w_gate, preferred_element_type=jnp.float32)
    upward = jnp.einsum("rd,edf->erf", features, w_up, preferred_element_type=jnp.float32)
    inner_act = (jax.nn.silu(gate_act) * upward).astype(jnp.bfloat16)
    produced = jnp.einsum("erf,efd->erd", inner_act, w_down, preferred_element_type=jnp.float32)
    moe_out = lax.psum_scatter(
        jnp.sum(local_mix.T[:, :, None] * produced, axis=0).T,
        ("seq", "head"),
        scatter_dimension=0,
        tiled=True,
    )
    mixed = (middle + moe_out.T).astype(jnp.bfloat16).reshape(step_count, REQS, -1)
    return (page_pool[None], mixed)


def solution(mesh):
    in_specs = (
        P(),
        P(),
        P(),
        P(),
        P(("seq", "head"), None, None, None),
        P(),
        P(),
        P(None, None, ("seq", "head")),
        P(None, ("seq", "head")),
        P(("seq", "head")),
        P(("seq", "head"), None),
        P(),
        P("seq", None, "head"),
        P("seq", None, "head"),
        P("seq", "head", None),
    )
    out_specs = (P("head", "seq", None, None), P(None, None, ("seq", "head")))
    return jax.shard_map(body, mesh=mesh, in_specs=in_specs, out_specs=out_specs, check_vma=False)
```

profile of v0, /device:TPU:0, one launch (start us, length us, event | category | flops | bytes accessed | tf_op | source)
XLA Modules:
  0.0 518.8 jit_solution(1423229279083668692)
XLA Ops:
  12.1 2.5 fusion.75
  16.1 2.0 fusion.10
  20.7 4.4 gather_fusion
  25.4 2.3 select_bitcast_fusion
  27.7 2.1 copy.100
  29.8 7.4 %all-to-all-start = ((bf16[32,3,64,256]{3,2,1,0:T(8,128)(2,1)}), bf16[32,3,64,256]{3,2,1,0:T(8,128)(2,1)}, u32[]{:S(2)}, u32[]{:S(2)}) async-start(bf16[32,3,64,256]{3,2,1,0:T(8,128)(2,1)} %bitcast.150), calls=%async_computation | async-start | bytes 6291456 | tf_op jit(solution)/shard_map/all_to_all | solution.py:162
  38.5 2.4 fusion.76
  41.2 115.7 %all_gather.13 = f32[32,2,16,32]{3,2,1,0:T(8,128)S(1)} all-gather(f32[1,2,16,32]{3,2,1,0:T(8,128)S(1)} %copy.112), channel_id=1, replica_groups=mesh['seq'=4,'head'=8] {'seq','head'}, dimensions={0}, use_global_device_ids=true | all-gather | bytes 135168 | tf_op jit(solution)/shard_map/all_gather | solution.py:19
  156.9 68.5 %all_gather.12 = f32[32,2,16,32]{3,2,1,0:T(8,128)S(1)} all-gather(f32[1,2,16,32]{3,2,1,0:T(8,128)S(1)} %copy.106), channel_id=1, replica_groups=mesh['seq'=4,'head'=8] {'seq','head'}, dimensions={0}, use_global_device_ids=true | all-gather | bytes 135168 | tf_op jit(solution)/shard_map/all_gather | solution.py:19
  226.6 49.5 %while.19 = (s32[]{:T(128)}, f32[2,16,32]{2,1,0:T(8,128)S(1)}, f32[2,16,32]{2,1,0:T(8,128)S(1)}, f32[2,16,32,128]{3,2,1,0:T(8,128)S(1)}, f32[32,2,16,32]{3,2,1,0...) while((s32[]{:T(128)}, f32[2,16,32]{2,1,0:T(8,128)S(1)}, ...), condition=%wide.region_9.10_spmd, body=%wide.region_8.9_spmd.sunk | while | flops 399365 | bytes 1613975 | solution.py:25
  228.2 1.5 fusion.87
  234.6 1.5 fusion.87
  245.8 1.5 fusion.87
  252.2 1.5 fusion.87
  258.6 1.5 fusion.87
  265.0 1.5 fusion.87
  279.1 36.9 %all-reduce = (f32[32]{0:T(128)S(1)}, f32[32,8]{0,1:T(8,128)S(1)}) all-reduce(f32[32]{0:T(128)S(1)} %get-tuple-element.237, f32[32,8]{0,1:T(8,128)S(1)} %fusion.48), channel_id=1, replica_groups=mesh['seq'=4,'head'=8] {'seq','head'}, use_global_device_ids=true, to_apply=%region_14.15 | all-reduce | flops 288 | bytes 2304 | tf_op jit(solution)/shard_map/psum | solution.py:217
  316.1 41.0 %all_gather.15 = bf16[32,4096]{1,0:T(8,128)(2,1)S(1)} all-gather(bf16[32,128]{1,0:T(8,128)(2,1)S(1)} %multiply_convert_fusion), channel_id=1, replica_groups=mesh['seq'=4,'head'=8] {'seq','head'}, dimensions={1}, use_global_device_ids=true | all-gather | bytes 270336 | tf_op jit(solution)/shard_map/all_gather | solution.py:227
  357.2 8.9 %convolution_bitcast_fusion.2 = f32[2,32,1024]{2,1,0:T(8,128)S(1)} fusion(bf16[2,4096,1024]{2,1,0:T(8,128)(2,1)} %param.29, bf16[32,4096]{1,0:T(8,128)(2,1)S(1)} %all_gather.15), kind=kOutput, calls=%fused_computation.30 | convolution fusion | flops 536870912 | bytes 17301504 | tf_op jit(solution)/shard_map/rd,edf->erf/dot_general | solution.py:231
  366.1 8.9 %fusion.25 = bf16[2,32,1024]{2,1,0:T(8,128)(2,1)S(1)} fusion(bf16[2,4096,1024]{2,1,0:T(8,128)(2,1)} %param.30, bf16[32,4096]{1,0:T(8,128)(2,1)S(1)} %all_gather.15, f32[2,32,1024]{2,1,0:T(8,128)S(1)} %convolution_bitcast_fusion.2), kind=kOutput, calls=%fused_computation.34 | convolution fusion | flops 537264128 | bytes 17432576 | tf_op jit(solution)/shard_map/rd,edf->erf/dot_general | solution.py:232
  375.1 3.8 fusion.9
  379.0 4.5 gather_fusion.1
  383.6 3.9 bitcast_select_fusion
  387.5 123.2 %reduce-scatter.2.cloned.1.call-done = f32[128,32]{0,1:T(8,128)} async-done(((f32[4096,32]{0,1:T(8,128)}), f32[128,32]{0,1:T(8,128)}) %reduce-scatter.2.cloned.1.call-update) | async-done | bytes 16400 | tf_op jit(solution)/shard_map/reduce_scatter | solution.py:235
  (165 shorter events, 55.7 us)
Async XLA Ops:
  7.2 271.4 %copy-start = (bf16[4096,128]{1,0:T(8,128)(2,1)S(1)}, bf16[4096,128]{1,0:T(8,128)(2,1)}, u32[]{:S(2)}) copy-start(bf16[4096,128]{1,0:T(8,128)(2,1)} %param.25) | copy-start | bytes 3145732
  7.2 218.3 %all-gather.2.cloned.1.call-start = ((), (), s32[]{:S(2)}) async-start(), calls=%async_computation.2 | async-start | bytes 17301504 | tf_op jit(solution)/shard_map/all_gather | solution.py:19
  16.1 3.7 copy-start.4
  29.8 8.7 %copy-start.2 = (bf16[2,16,8,256]{3,2,1,0:T(8,128)(2,1)S(1)}, bf16[2,16,8,256]{3,2,1,0:T(8,128)(2,1)}, u32[]{:S(2)}) copy-start(bf16[2,16,8,256]{3,2,1,0:T(8,128)(2,1)} %param.23) | copy-start | bytes 393220
  29.8 349.2 %all-to-all-start = ((bf16[32,3,64,256]{3,2,1,0:T(8,128)(2,1)}), bf16[32,3,64,256]{3,2,1,0:T(8,128)(2,1)}, u32[]{:S(2)}, u32[]{:S(2)}) async-start(bf16[32,3,64,256]{3,2,1,0:T(8,128)(2,1)} %bitcast.150), calls=%async_computation | async-start | bytes 6291456 | tf_op jit(solution)/shard_map/all_to_all | solution.py:162
  37.2 3.9 copy-start.7
  37.2 3.9 copy-start.6
  37.2 473.4 %reduce-scatter.2.cloned.1.call-start = ((), (), s32[]{:S(2)}) async-start(), calls=%async_computation.3 | async-start | bytes 540672 | tf_op jit(solution)/shard_map/reduce_scatter | solution.py:235
  276.1 2.4 copy-start.3
  277.0 2.0 copy-start.5
  357.2 17.8 %slice-start = ((s8[16777216]{0:T(1024)(128)(4,1)}), s8[4194304]{0:T(1024)(128)(4,1)S(1)}, s32[]{:S(2)}) async-start(s8[16777216]{0:T(1024)(128)(4,1)} %bitcast.148), calls=%async_computation.4 | async-start | bytes 8388608
  357.2 17.8 %slice-start.1 = ((s8[16777216]{0:T(1024)(128)(4,1)}), s8[4194304]{0:T(1024)(128)(4,1)S(1)}, s32[]{:S(2)}) async-start(s8[16777216]{0:T(1024)(128)(4,1)} %bitcast.148), calls=%async_computation.5 | async-start | bytes 8388608
  366.1 9.0 %slice-start.2 = ((s8[16777216]{0:T(1024)(128)(4,1)}), s8[4194304]{0:T(1024)(128)(4,1)S(1)}, s32[]{:S(2)}) async-start(s8[16777216]{0:T(1024)(128)(4,1)} %bitcast.148), calls=%async_computation.6 | async-start | bytes 8388608
  366.1 9.0 %slice-start.3 = ((s8[16777216]{0:T(1024)(128)(4,1)}), s8[4194304]{0:T(1024)(128)(4,1)S(1)}, s32[]{:S(2)}) async-start(s8[16777216]{0:T(1024)(128)(4,1)} %bitcast.148), calls=%async_computation.7 | async-start | bytes 8388608
  379.0 132.9 %copy-start.1 = (bf16[4096,128]{1,0:T(8,128)(2,1)S(1)}, bf16[4096,128]{1,0:T(8,128)(2,1)}, u32[]{:S(2)}) copy-start(bf16[4096,128]{1,0:T(8,128)(2,1)} %param.25) | copy-start | bytes 3145732
Sparse Core Ops, SparseCore 0:
  19.9 166.8 all-gather.1
  379.0 131.6 reduce-scatter.1
where the time goes:
time: 521 us; the launch traced here: 519 us
  blocking collectives  262 us (50%)
  waiting for transfers between devices  123 us (24%)
  other arithmetic  60.5 us (12%)
  matrix products  30.4 us (6%)
  local copies, waits for them, and re-layouts  19.7 us (4%)
  between operations  14.5 us (3%)
  starting transfers between devices  7.51 us (1%)
    all_gather x2, blocking collectives, joined(): everything = jax.tree.map(lambda part: lax.all_gather(part, axis), array)  184 us
    reduce_scatter x1, waiting for transfers between devices, body(): lax.psum_scatter(jnp.sum(local_mix.T[:, :, None] * produced, axis=0).T, (...  123 us
    add x31, other arithmetic, combine(): first_acc * first_factor[..., None] + second_acc * second_factor[..., None]  47.9 us
    all_gather x1, blocking collectives, body(): features = lax.all_gather(normed, ('seq', 'head'), axis=1, tiled=True)  41 us
    psum x1, blocking collectives, body(): lax.psum((jnp.sum(middle * middle, axis=1), jnp.dot(middle * gain_row, ro...  36.9 us
  transfers between devices with their start and end apart: 3, of which 1 were waited for; matrix products, arithmetic and copies ran while one was open for 19% of the time, Pallas kernels for 0%

commit v1 on v0

--- a/solution.py
+++ b/solution.py
@@ -215,11 +215,14 @@
     middle = hidden_in.reshape(row_count, -1).astype(jnp.float32) + attn_out
     gain_row = norm_gain.astype(jnp.float32)[None, :]
     squares, routed = lax.psum(
-        (
-            jnp.sum(middle * middle, axis=1),
-            jnp.dot(middle * gain_row, router.astype(jnp.float32), precision=HIGHEST),
+        lax.psum(
+            (
+                jnp.sum(middle * middle, axis=1),
+                jnp.dot(middle * gain_row, router.astype(jnp.float32), precision=HIGHEST),
+            ),
+            "head",
         ),
-        ("seq", "head"),
+        "seq",
     )
     inverse_rms = lax.rsqrt(squares / D + EPSILON)
     logits = routed * inverse_rms[:, None]

time: 521 us -> 503 us (0.965)
  blocking collectives: 262 us -> 243 us
    psum x1, blocking collectives: 36.9 us -> 12.4 us  [body(): lax.psum((jnp.sum(middle * middle, axis=1), jnp.dot(middle * gain_row, ro...]
    psum x0 -> x1, blocking collectives: none -> 8.51 us  [body(): lax.psum(lax.psum((jnp.sum(middle * middle, axis=1), jnp.dot(middle * gai...]
where the time goes in v1:
time: 503 us; the launch traced here: 501 us
  blocking collectives  243 us (48%)
  waiting for transfers between devices  125 us (25%)
  other arithmetic  60.5 us (12%)
  matrix products  30.4 us (6%)
  local copies, waits for them, and re-layouts  19.7 us (4%)
  between operations  14.5 us (3%)
  starting transfers between devices  7.51 us (1%)
    all_gather x2, blocking collectives, joined(): everything = jax.tree.map(lambda part: lax.all_gather(part, axis), array)  184 us
    reduce_scatter x1, waiting for transfers between devices, body(): lax.psum_scatter(jnp.sum(local_mix.T[:, :, None] * produced, axis=0).T, (...  125 us
    add x31, other arithmetic, combine(): first_acc * first_factor[..., None] + second_acc * second_factor[..., None]  47.9 us
    all_gather x1, blocking collectives, body(): features = lax.all_gather(normed, ('seq', 'head'), axis=1, tiled=True)  37.6 us
    psum x1, blocking collectives, body(): lax.psum((jnp.sum(middle * middle, axis=1), jnp.dot(middle * gain_row, ro...  12.4 us
  transfers between devices with their start and end apart: 3, of which 1 were waited for; matrix products, arithmetic and copies ran while one was open for 19% of the time, Pallas kernels for 0%

profile of v1, /device:TPU:0, one launch (start us, length us, event | category | flops | bytes accessed | tf_op | source)
XLA Modules:
  0.0 500.9 jit_solution(17140045065388001763)
XLA Ops:
  12.1 2.5 fusion.75
  16.1 2.0 fusion.10
  20.7 4.4 gather_fusion
  25.4 2.3 select_bitcast_fusion
  27.7 2.1 copy.100
  29.8 7.4 %all-to-all-start = ((bf16[32,3,64,256]{3,2,1,0:T(8,128)(2,1)}), bf16[32,3,64,256]{3,2,1,0:T(8,128)(2,1)}, u32[]{:S(2)}, u32[]{:S(2)}) async-start(bf16[32,3,64,256]{3,2,1,0:T(8,128)(2,1)} %bitcast.150), calls=%async_computation | async-start | bytes 6291456 | tf_op jit(solution)/shard_map/all_to_all | solution.py:162
  38.5 2.4 fusion.76
  41.2 115.7 %all_gather.13 = f32[32,2,16,32]{3,2,1,0:T(8,128)S(1)} all-gather(f32[1,2,16,32]{3,2,1,0:T(8,128)S(1)} %copy.112), channel_id=1, replica_groups=mesh['seq'=4,'head'=8] {'seq','head'}, dimensions={0}, use_global_device_ids=true | all-gather | bytes 135168 | tf_op jit(solution)/shard_map/all_gather | solution.py:19
  156.9 68.5 %all_gather.12 = f32[32,2,16,32]{3,2,1,0:T(8,128)S(1)} all-gather(f32[1,2,16,32]{3,2,1,0:T(8,128)S(1)} %copy.106), channel_id=1, replica_groups=mesh['seq'=4,'head'=8] {'seq','head'}, dimensions={0}, use_global_device_ids=true | all-gather | bytes 135168 | tf_op jit(solution)/shard_map/all_gather | solution.py:19
  226.6 49.5 %while.19 = (s32[]{:T(128)}, f32[2,16,32]{2,1,0:T(8,128)S(1)}, f32[2,16,32]{2,1,0:T(8,128)S(1)}, f32[2,16,32,128]{3,2,1,0:T(8,128)S(1)}, f32[32,2,16,32]{3,2,1,0...) while((s32[]{:T(128)}, f32[2,16,32]{2,1,0:T(8,128)S(1)}, ...), condition=%wide.region_9.10_spmd, body=%wide.region_8.9_spmd.sunk | while | flops 399365 | bytes 1613975 | solution.py:25
  228.2 1.5 fusion.87
  234.6 1.5 fusion.87
  245.8 1.5 fusion.87
  252.2 1.5 fusion.87
  258.6 1.5 fusion.87
  279.1 12.4 %all-reduce = (f32[32]{0:T(128)S(1)}, f32[32,8]{0,1:T(8,128)S(1)}) all-reduce(f32[32]{0:T(128)S(1)} %get-tuple-element.239, f32[32,8]{0,1:T(8,128)S(1)} %fusion.48), channel_id=1, replica_groups=mesh['seq'=4,'head'=8] {'head'}, use_global_device_ids=true, to_apply=%region_15.16 | all-reduce | flops 288 | bytes 2304 | tf_op jit(solution)/shard_map/psum | solution.py:218
  291.5 8.5 %all-reduce.1 = (f32[32]{0:T(128)S(1)}, f32[32,8]{0,1:T(8,128)S(1)}) all-reduce(f32[32]{0:T(128)S(1)} %get-tuple-element.213, f32[32,8]{0,1:T(8,128)S(1)} %get-tuple-element.214), channel_id=1, replica_groups=mesh['seq'=4,'head'=8] {'seq'}, use_global_device_ids=true, to_apply=%region_16.17 | all-reduce | flops 288 | bytes 2304 | tf_op jit(solution)/shard_map/psum | solution.py:217
  300.2 37.6 %all_gather.15 = bf16[32,4096]{1,0:T(8,128)(2,1)S(1)} all-gather(bf16[32,128]{1,0:T(8,128)(2,1)S(1)} %multiply_convert_fusion), channel_id=1, replica_groups=mesh['seq'=4,'head'=8] {'seq','head'}, dimensions={1}, use_global_device_ids=true | all-gather | bytes 270336 | tf_op jit(solution)/shard_map/all_gather | solution.py:230
  337.8 8.9 %convolution_bitcast_fusion.2 = f32[2,32,1024]{2,1,0:T(8,128)S(1)} fusion(bf16[2,4096,1024]{2,1,0:T(8,128)(2,1)} %param.29, bf16[32,4096]{1,0:T(8,128)(2,1)S(1)} %all_gather.15), kind=kOutput, calls=%fused_computation.30 | convolution fusion | flops 536870912 | bytes 17301504 | tf_op jit(solution)/shard_map/rd,edf->erf/dot_general | solution.py:234
  346.7 8.9 %fusion.25 = bf16[2,32,1024]{2,1,0:T(8,128)(2,1)S(1)} fusion(bf16[2,4096,1024]{2,1,0:T(8,128)(2,1)} %param.30, bf16[32,4096]{1,0:T(8,128)(2,1)S(1)} %all_gather.15, f32[2,32,1024]{2,1,0:T(8,128)S(1)} %convolution_bitcast_fusion.2), kind=kOutput, calls=%fused_computation.34 | convolution fusion | flops 537264128 | bytes 17432576 | tf_op jit(solution)/shard_map/rd,edf->erf/dot_general | solution.py:235
  355.7 3.8 fusion.9
  359.7 4.5 gather_fusion.1
  364.2 3.9 bitcast_select_fusion
  368.1 124.6 %reduce-scatter.2.cloned.1.call-done = f32[128,32]{0,1:T(8,128)} async-done(((f32[4096,32]{0,1:T(8,128)}), f32[128,32]{0,1:T(8,128)}) %reduce-scatter.2.cloned.1.call-update) | async-done | bytes 16400 | tf_op jit(solution)/shard_map/reduce_scatter | solution.py:238
  (166 shorter events, 57.2 us)
Async XLA Ops:
  7.2 271.4 %copy-start = (bf16[4096,128]{1,0:T(8,128)(2,1)S(1)}, bf16[4096,128]{1,0:T(8,128)(2,1)}, u32[]{:S(2)}) copy-start(bf16[4096,128]{1,0:T(8,128)(2,1)} %param.25) | copy-start | bytes 3145732
  7.2 218.3 %all-gather.2.cloned.1.call-start = ((), (), s32[]{:S(2)}) async-start(), calls=%async_computation.2 | async-start | bytes 17301504 | tf_op jit(solution)/shard_map/all_gather | solution.py:19
  16.1 3.7 copy-start.4
  29.8 8.7 %copy-start.2 = (bf16[2,16,8,256]{3,2,1,0:T(8,128)(2,1)S(1)}, bf16[2,16,8,256]{3,2,1,0:T(8,128)(2,1)}, u32[]{:S(2)}) copy-start(bf16[2,16,8,256]{3,2,1,0:T(8,128)(2,1)} %param.23) | copy-start | bytes 393220
  29.8 329.9 %all-to-all-start = ((bf16[32,3,64,256]{3,2,1,0:T(8,128)(2,1)}), bf16[32,3,64,256]{3,2,1,0:T(8,128)(2,1)}, u32[]{:S(2)}, u32[]{:S(2)}) async-start(bf16[32,3,64,256]{3,2,1,0:T(8,128)(2,1)} %bitcast.150), calls=%async_computation | async-start | bytes 6291456 | tf_op jit(solution)/shard_map/all_to_all | solution.py:162
  37.2 3.9 copy-start.7
  37.2 3.9 copy-start.6
  37.2 455.5 %reduce-scatter.2.cloned.1.call-start = ((), (), s32[]{:S(2)}) async-start(), calls=%async_computation.3 | async-start | bytes 540672 | tf_op jit(solution)/shard_map/reduce_scatter | solution.py:238
  276.1 2.4 copy-start.3
  277.0 2.0 copy-start.5
  337.8 17.8 %slice-start = ((s8[16777216]{0:T(1024)(128)(4,1)}), s8[4194304]{0:T(1024)(128)(4,1)S(1)}, s32[]{:S(2)}) async-start(s8[16777216]{0:T(1024)(128)(4,1)} %bitcast.148), calls=%async_computation.4 | async-start | bytes 8388608
  337.8 17.8 %slice-start.1 = ((s8[16777216]{0:T(1024)(128)(4,1)}), s8[4194304]{0:T(1024)(128)(4,1)S(1)}, s32[]{:S(2)}) async-start(s8[16777216]{0:T(1024)(128)(4,1)} %bitcast.148), calls=%async_computation.5 | async-start | bytes 8388608
  346.7 9.0 %slice-start.2 = ((s8[16777216]{0:T(1024)(128)(4,1)}), s8[4194304]{0:T(1024)(128)(4,1)S(1)}, s32[]{:S(2)}) async-start(s8[16777216]{0:T(1024)(128)(4,1)} %bitcast.148), calls=%async_computation.6 | async-start | bytes 8388608
  346.7 9.0 %slice-start.3 = ((s8[16777216]{0:T(1024)(128)(4,1)}), s8[4194304]{0:T(1024)(128)(4,1)S(1)}, s32[]{:S(2)}) async-start(s8[16777216]{0:T(1024)(128)(4,1)} %bitcast.148), calls=%async_computation.7 | async-start | bytes 8388608
  359.7 134.4 %copy-start.1 = (bf16[4096,128]{1,0:T(8,128)(2,1)S(1)}, bf16[4096,128]{1,0:T(8,128)(2,1)}, u32[]{:S(2)}) copy-start(bf16[4096,128]{1,0:T(8,128)(2,1)} %param.25) | copy-start | bytes 3145732
Sparse Core Ops, SparseCore 0:
  19.9 166.8 all-gather.1
  359.6 133.0 reduce-scatter.1
